TPU v7x, 32 devices: a whole 2x2x4 slice. The times are simulated.
32 devices in a mesh: row: 4 (over x, core), col: 8 (over z, y).
Axes of the slice: x: 2, y: 2, z: 4, core: 2. Of those that a mesh axis runs over, the one named last changes fastest.
Arguments:
- front_panels: float32 [16, 4, 256, 8, 8, 256], P(None, 'row', 'col'), as said below
- child_update_tiles: float32 [4, 8, 8, 256, 256], P('row', 'col'), may hold values from -2 to 2
- child_rows: int32 [4, 8, 8], P('row', 'col'), may hold values from 0 to 63, as said below
- child_cols: int32 [4, 8, 8], P('row', 'col'), may hold values from 0 to 7
- child_counts: int32 [4, 8], P('row', 'col'), may hold values from 4 to 8, as said below
- row_maps: int32 [4, 8, 8, 256], P('row', 'col'), may hold values from 0 to 255, each once within a row
- col_maps: int32 [4, 8, 8, 256], P('row', 'col'), may hold values from 0 to 255, each once within a row
Outputs:
- factored_front: float32 [16, 4, 256, 8, 8, 256], P(None, 'row', None, None, 'col')
Inputs may be any that keep to these rules, and one draw needn't show every extreme that they name: child_rows[r, c, k] modulo 4 names one of four owner rows; among the live slots of one device at most 2 name the same owner row, and some device sends exactly 2 to some owner; every slot's target tile column is at most its target tile row. `child_counts`: every device of col index 0 has all slots live. `front_panels`: the diagonal of the front dominates its first tile, so that tile stays positive definite after the children are added.
All inputs are finite; a program needn't handle non-finite values.
Results may differ from a plain program's by a relative error of at most 0.0003.
Values sent between devices are 32-bit elements; how exact they have to be, the bound alone decides.
No kernel may reach another device: no remote copies, remote signals or barrier semaphores. Data moves between devices by JAX's collectives and lax.ppermute only.
A program may use at most 320 MiB of HBM per device.

v0:
```python
import jax
import jax.numpy as jnp
from jax import lax
from jax.sharding import PartitionSpec as P


def broadcast(value, axis, source):
    kept = jnp.where(lax.axis_index(axis) == source, value, 0).astype(value.dtype)
    return lax.psum(kept, axis)


def slot_positions(owners, is_live):
    slot_entries = owners.shape[-1]
    earlier = lax.broadcasted_iota(
        jnp.int32, (slot_entries, slot_entries), 0
    ) < lax.broadcasted_iota(jnp.int32, (slot_entries, slot_entries), 1)
    same_owner = (owners[..., :, None] == owners[..., None, :]) & is_live[..., :, None] & earlier
    return jnp.sum(same_owner.astype(jnp.int32), axis=-2)


def on_device(
    front_panels, child_update_tiles, child_rows, child_cols, child_counts, row_maps, col_maps
):
    largest_index = lax.Precision.HIGHEST
    row_size = lax.axis_size("row")
    col_size = lax.axis_size("col")
    my_row = lax.axis_index("row")
    my_col = lax.axis_index("col")
    front_width = front_panels.shape[-1]
    blocks = lax.all_to_all(front_panels, "col", split_axis=4, concat_axis=2, tiled=True)
    row_tiles = blocks.shape[0]
    col_tiles = blocks.shape[3]
    blocks = blocks.reshape(row_tiles, front_width, col_tiles, front_width)
    slot_entries = child_update_tiles.shape[2]
    capacity = slot_entries // 4
    labels = lax.broadcasted_iota(jnp.int32, (1, 1, front_width), 2)
    row_indicator = (row_maps.reshape(slot_entries, front_width)[:, :, None] == labels).astype(
        jnp.float32
    )
    column_indicator = (col_maps.reshape(slot_entries, front_width)[:, :, None] == labels).astype(
        jnp.float32
    )
    shifted_tiles = jnp.einsum(
        "gml,gmq->glq",
        row_indicator,
        child_update_tiles.reshape(slot_entries, front_width, front_width),
        precision=largest_index,
    )
    shifted_tiles = jnp.einsum(
        "afb,abx->afx", shifted_tiles, column_indicator, precision=largest_index
    )
    slot_ids = lax.broadcasted_iota(jnp.int32, (slot_entries,), 0)
    is_live = slot_ids < child_counts.reshape(())
    owners = child_rows.reshape(slot_entries) % row_size
    positions = slot_positions(owners, is_live)
    dest_ids = lax.broadcasted_iota(jnp.int32, (row_size, capacity, slot_entries), 0)
    place_ids = lax.broadcasted_iota(jnp.int32, (row_size, capacity, slot_entries), 1)
    selector = (
        (owners[None, None, :] == dest_ids)
        & (positions[None, None, :] == place_ids)
        & is_live[None, None, :]
    ).astype(jnp.float32)
    outgoing = jnp.einsum(
        "opk,kx->opx",
        selector,
        shifted_tiles.reshape(slot_entries, front_width * front_width),
        precision=largest_index,
    )
    incoming = lax.all_to_all(outgoing, "row", split_axis=0, concat_axis=0, tiled=True)
    all_rows, all_cols, all_counts = (
        lax.all_gather(child_rows, "row", axis=0, tiled=True),
        lax.all_gather(child_cols, "row", axis=0, tiled=True),
        lax.all_gather(child_counts, "row", axis=0, tiled=True),
    )
    source_rows = all_rows.reshape(row_size, slot_entries)
    source_cols = all_cols.reshape(row_size, slot_entries)
    source_live = slot_ids[None, :] < all_counts.reshape(row_size)[:, None]
    source_owner = source_rows % row_size
    source_pos = slot_positions(source_owner, source_live)
    mine = (source_live & (source_owner == my_row)).astype(jnp.float32)
    depth_onehot = (
        (source_rows // row_size)[:, :, None]
        == lax.broadcasted_iota(jnp.int32, (1, 1, row_tiles), 2)
    ).astype(jnp.float32) * mine[:, :, None]
    across_onehot = (
        source_cols[:, :, None] == lax.broadcasted_iota(jnp.int32, (1, 1, col_tiles), 2)
    ).astype(jnp.float32)
    place_onehot = (
        source_pos[:, :, None] == lax.broadcasted_iota(jnp.int32, (1, 1, capacity), 2)
    ).astype(jnp.float32)
    landing = jnp.einsum(
        "ska,skb,skp->absp", depth_onehot, across_onehot, place_onehot, precision=largest_index
    )
    incoming = incoming.reshape(row_size, capacity, front_width, front_width)
    blocks = blocks + jnp.einsum("absp,spxy->axby", landing, incoming, precision=largest_index)
    tile_i = lax.broadcasted_iota(jnp.int32, (row_tiles, 1, col_tiles, 1), 0) * row_size + my_row
    tile_j = lax.broadcasted_iota(jnp.int32, (row_tiles, 1, col_tiles, 1), 2) * col_size + my_col
    flipped = jnp.einsum("axby->aybx", blocks)
    blocks = jnp.where(tile_i == tile_j, 0.5 * (blocks + flipped), blocks)
    identity = jnp.eye(front_width, dtype=jnp.float32)
    corner = blocks[0, :, 0, :]
    at_root = (my_row == 0) & (my_col == 0)
    factor = jnp.linalg.cholesky(jnp.where(at_root, corner, identity))
    factor = broadcast(factor, "row", 0)
    column = blocks[:, :, 0, :].reshape(row_tiles * front_width, front_width)
    solved = jax.scipy.linalg.solve_triangular(factor, column.T, lower=True).T.reshape(
        row_tiles, front_width, front_width
    )
    tile_index = lax.broadcasted_iota(jnp.int32, (row_tiles, 1, 1), 0) * row_size + my_row
    kept = jnp.where(tile_index == 0, factor[None, :, :], solved)
    below = jnp.where(tile_index == 0, 0.0, solved)
    row_panel = broadcast(below, "col", 0)
    group = col_size // row_size
    whole = lax.all_gather(row_panel, "row", axis=0, tiled=True)
    whole = whole.reshape(row_size, col_tiles, group, front_width, front_width)
    picked = lax.dynamic_index_in_dim(whole, my_col % row_size, 0, keepdims=False)
    col_panel = lax.dynamic_index_in_dim(picked, my_col // row_size, 1, keepdims=False)
    blocks = blocks - jnp.einsum("asx,bqx->asbq", row_panel, col_panel, precision=largest_index)
    first_column = jnp.where(my_col == 0, kept, blocks[:, :, 0, :])
    blocks = blocks.at[:, :, 0, :].set(first_column)
    blocks = jnp.where(tile_i >= tile_j, blocks, 0.0)
    return blocks.reshape(row_tiles, 1, front_width, col_tiles, 1, front_width)


def solution(mesh):
    return jax.shard_map(
        on_device,
        mesh=mesh,
        in_specs=(
            P(None, "row", "col", None, None, None),
            P("row", "col", None, None, None),
            P("row", "col", None),
            P("row", "col", None),
            P("row", "col"),
            P("row", "col", None, None),
            P("row", "col", None, None),
        ),
        out_specs=P(None, "row", None, None, "col", None),
        check_vma=False,
    )
```

profile of v0, /device:TPU:0, one launch (start us, length us, event | category | flops | bytes accessed | tf_op | source)
XLA Modules:
  0.0 1470.2 jit_solution(9605571834959242759)
XLA Ops:
  15.7 4.1 fusion.33
  19.8 4.2 all-to-all-start.1
  24.0 30.6 %copy.67 = f32[16,1,32,8,8,256]{5,3,2,0,1,4:T(8,128)} copy(f32[16,1,32,8,8,256]{5,4,3,2,1,0:T(8,128)} %param.9) | data formatting | bytes 67108864 | tf_op args[0]
  55.9 7.1 all-to-all-start
  64.2 5.8 all-reduce.1
  70.0 5.0 all_gather.14
  75.0 5.2 all_gather.17
  84.8 30.9 %convolution_bitcast_fusion = f32[256,256,16,8]{1,2,3,0:T(8,128)} fusion(f32[4,2,256,256,1]{3,2,1,0,4:T(8,128)S(1)} %bitcast.110, f32[16,8,4,2]{0,1,3,2:T(8,128)S(1)} %convolution_bitcast_fusion.1), kind=kOutput, calls=%fused_computation.8 | convolution fusion | flops 805306368 | bytes 35655680 | tf_op jit(solution)/shard_map/absp,spxy->axby/dot_general | solution.py:95
  115.7 34.4 %copy.72 = f32[256,256,16,8]{0,1,3,2:T(8,128)} copy(f32[256,256,16,8]{1,2,3,0:T(8,128)} %convolution_bitcast_fusion) | data formatting | bytes 67108864 | tf_op jit(solution)/shard_map/absp,spxy->axby/dot_general | solution.py:95
  150.2 637.7 %all-to-all-done = f32[16,1,32,8,8,256]{5,3,2,0,1,4:T(8,128)} async-done(((f32[16,1,32,8,8,256]{5,3,2,0,1,4:T(8,128)}), f32[16,1,32,8,8,256]{5,3,2,0,1,4:T(8,128)}, u32[]{:S(2)}, u32[]{:S(2)}) %all-to-all-start) | async-done | bytes 33554464 | tf_op jit(solution)/shard_map/all_to_all | solution.py:30
  787.9 22.9 %copy.68 = f32[16,1,32,8,8,256]{5,3,2,4,0,1:T(8,128)} copy(f32[16,1,32,8,8,256]{5,3,2,0,1,4:T(8,128)} %all-to-all-done) | data formatting | bytes 67108864 | tf_op jit(solution)/shard_map/all_to_all | solution.py:30
  810.7 35.0 %copy.73 = f32[16,256,8,256]{1,3,2,0:T(8,128)} copy(f32[16,256,8,256]{3,2,1,0:T(8,128)} %bitcast.104) | data formatting | bytes 67108864 | tf_op jit(solution)/shard_map/reshape | solution.py:33
  845.7 33.5 %bitcast_add_fusion.1 = f32[16,256,8,256]{1,3,2,0:T(8,128)} fusion(f32[16,256,8,256]{1,3,2,0:T(8,128)} %copy.73, f32[256,256,16,8]{0,1,3,2:T(8,128)} %copy.72), kind=kLoop, calls=%fused_computation.5 | loop fusion | flops 8388608 | bytes 100663296 | tf_op jit(solution)/shard_map/add | solution.py:95
  879.2 31.9 %copy.74 = f32[16,256,8,256]{3,1,2,0:T(8,128)} copy(f32[16,256,8,256]{1,3,2,0:T(8,128)} %bitcast_add_fusion.1) | data formatting | bytes 67108864 | tf_op jit(solution)/shard_map/add | solution.py:95
  911.2 33.6 %fusion.1 = f32[16,256,8,256]{1,3,2,0:T(8,128)} fusion(f32[16,256,8,256]{1,3,2,0:T(8,128)} %bitcast_add_fusion.1, f32[16,256,8,256]{3,1,2,0:T(8,128)} %copy.74, pred[16,8]{1,0:T(8,128)(4,1)S(1)} %get-tuple-element.42), kind=kLoop, calls=%fused_computation.4 | loop fusion | flops 25165824 | bytes 100663424 | tf_op jit(solution)/shard_map/jit(_where)/select_n | solution.py:99
  947.0 11.7 cholesky.50
  958.7 9.8 custom-call.15
  969.0 11.7 cholesky.105
  983.6 4.5 slice.96
  988.1 5.8 copy.76
  993.9 5.7 copy.77
  999.6 14.6 all-reduce.5.cloned.1.call-done
  1019.0 19.7 %custom-call.16 = f32[2,128,128]{1,2,0:T(8,128)S(1)} custom-call(f32[2,128,128]{2,1,0:T(8,128)S(1)} %get-tuple-element.24), custom_call_target="InvertDiagBlocksLowerTriangular" | custom-call | tf_op jit(solution)/shard_map/jit(_solve_triangular)/triangular_solve | solution.py:106
  1048.6 5.6 copy.94
  1054.2 4.7 select_select_fusion
  1059.0 156.4 %all-reduce.7.cloned.1.call-done = f32[16,256,256]{2,1,0:T(8,128)} async-done(((f32[16,256,256]{2,1,0:T(8,128)}), f32[16,256,256]{2,1,0:T(8,128)}) %all-reduce.7.cloned.1.call-update) | async-done | bytes 4194320 | tf_op jit(solution)/shard_map/psum | solution.py:9
  1215.5 5.6 copy.83
  1221.2 100.9 %all-gather.2.cloned.1.call-done = f32[64,256,256]{2,1,0:T(8,128)} async-done(((f32[16,256,256]{2,1,0:T(8,128)}), f32[64,256,256]{2,1,0:T(8,128)}) %all-gather.2.cloned.1.call-update) | async-done | bytes 16777232 | tf_op jit(solution)/shard_map/all_gather | solution.py:114
  1322.0 35.3 %convolution_subtract_fusion = f32[16,256,8,256]{1,3,2,0:T(8,128)} fusion(f32[16,256,8,256]{1,3,2,0:T(8,128)} %fusion.1, f32[16,256,256]{2,1,0:T(8,128)} %all-reduce.7.cloned.1.call-done, f32[4,8,2,256,256]{4,3,2,1,0:T(8,128)} %bitcast.111, s32[]{:T(128)S(6)} %select_n.139, s32[]{:T(128)S(6)} %select_n.142), kind=kOutput, calls=%fused_computation.7 | convolution fusion | flops 25778192384 | bytes 73400328 | tf_op jit(solution)/shard_map/asx,bqx->asbq/dot_general | solution.py:118
  1357.3 4.8 fusion.2
  1362.2 22.9 %select_bitcast_fusion = f32[16,1,256,8,1,256]{2,5,3,0,4,1:T(8,128)} fusion(f32[16,256,8,256]{1,3,2,0:T(8,128)} %fusion.2, pred[16,8]{1,0:T(8,128)(4,1)S(1)} %copy-done.6), kind=kLoop, calls=%fused_computation.6 | loop fusion | flops 8388608 | bytes 67108992 | tf_op jit(solution)/shard_map/reshape | solution.py:122
  1385.1 78.3 %copy.84 = f32[16,1,256,8,1,256]{5,4,3,2,1,0:T(1,128)} copy(f32[16,1,256,8,1,256]{2,5,3,0,4,1:T(8,128)} %select_bitcast_fusion) | data formatting | bytes 67108864 | tf_op jit(solution)/shard_map/reshape | solution.py:122
  (80 shorter events, 38.6 us)
Async XLA Ops:
  6.5 1.6 copy-start
  6.5 3.8 copy-start.7
  19.8 34.8 %all-to-all-start.1 = ((f32[4,2,65536]{2,1,0:T(2,128)}), f32[4,2,65536]{2,1,0:T(2,128)S(1)}, u32[]{:S(2)}, u32[]{:S(2)}) async-start(f32[4,2,65536]{2,1,0:T(2,128)} %fusion.33), calls=%async_computation.1 | async-start | bytes 4194304 | tf_op jit(solution)/shard_map/all_to_all | solution.py:69
  54.6 8.5 copy-start.10
  54.6 15.4 %copy-start.8 = (s32[1,1,8]{2,1,0:T(1,128)S(1)}, s32[1,1,8]{2,1,0:T(1,128)}, u32[]{:S(2)}) copy-start(s32[1,1,8]{2,1,0:T(1,128)} %param.11) | copy-start | bytes 100
  54.6 20.5 %copy-start.9 = (s32[1,1,8]{2,1,0:T(1,128)S(1)}, s32[1,1,8]{2,1,0:T(1,128)}, u32[]{:S(2)}) copy-start(s32[1,1,8]{2,1,0:T(1,128)} %param.12) | copy-start | bytes 100
  54.6 1.3 copy-start.4
  55.9 731.9 %all-to-all-start = ((f32[16,1,32,8,8,256]{5,3,2,0,1,4:T(8,128)}), f32[16,1,32,8,8,256]{5,3,2,0,1,4:T(8,128)}, u32[]{:S(2)}, u32[]{:S(2)}) async-start(f32[16,1,32,8,8,256]{5,3,2,0,1,4:T(8,128)} %copy.67), calls=%async_computation | async-start | bytes 67108864 | tf_op jit(solution)/shard_map/all_to_all | solution.py:30
  63.0 951.1 %all-reduce.5.cloned.1.call-start = ((), (), s32[]{:S(2)}) async-start(), calls=%async_computation.2 | async-start | bytes 524288 | tf_op jit(solution)/shard_map/psum | solution.py:9
  983.5 231.9 %all-reduce.7.cloned.1.call-start = ((), (), s32[]{:S(2)}) async-start(), calls=%async_computation.3 | async-start | bytes 8388608 | tf_op jit(solution)/shard_map/psum | solution.py:9
  1038.7 3.7 copy-start.3
  1059.0 263.1 %all-gather.2.cloned.1.call-start = ((), (), s32[]{:S(2)}) async-start(), calls=%async_computation.4 | async-start | bytes 20971520 | tf_op jit(solution)/shard_map/all_gather | solution.py:114
  1215.5 5.6 copy-start.5
  1322.0 35.3 %copy-start.2 = (f32[16,256,1,256]{1,3,2,0:T(8,128)S(1)}, f32[16,256,1,256]{1,3,2,0:T(8,128)}, u32[]{:S(2)}) copy-start(f32[16,256,1,256]{1,3,2,0:T(8,128)} %copy.83) | copy-start | bytes 12582916
  1357.3 4.8 copy-start.6
  1385.1 78.3 %copy-start.1 = (f32[1,1,8,256,256]{4,3,2,1,0:T(8,128)S(1)}, f32[1,1,8,256,256]{4,3,2,1,0:T(8,128)}, u32[]{:S(2)}) copy-start(f32[1,1,8,256,256]{4,3,2,1,0:T(8,128)} %param.10) | copy-start | bytes 6291460
Sparse Core Ops, SparseCore 0:
  983.6 30.4 all-reduce.4
  1059.1 156.2 all-reduce.6
  1217.1 104.9 all-gather.1
where the time goes:
time: 1480 us; the launch traced here: 1470 us
  waiting for transfers between devices  910 us (61%)
  local copies, waits for them, and re-layouts  273 us (18%)
  other arithmetic  162 us (11%)
  matrix products  83.3 us (6%)
  blocking collectives  16 us (1%)
  between operations  15.5 us (1%)
    all_to_all x1, waiting for transfers between devices, on_device(): lax.all_to_all(front_panels, 'col', split_axis=4, concat_axis=2, tiled=True)  638 us
    psum x2, waiting for transfers between devices, broadcast(): return lax.psum(kept, axis)  171 us
    all_gather x1, waiting for transfers between devices, on_device(): whole = lax.all_gather(row_panel, 'row', axis=0, tiled=True)  101 us
    reshape x1, local copies, waits for them, and re-layouts, on_device(): return blocks.reshape(row_tiles, 1, front_width, col_tiles, 1, front_width)  78.3 us
    dot_general x1, matrix products, on_device(): jnp.einsum('asx,bqx->asbq', row_panel, col_panel, precision=largest_index)  35.3 us
    reshape x1, local copies, waits for them, and re-layouts, on_device(): blocks = blocks.reshape(row_tiles, front_width, col_tiles, front_width)  35 us
    dot_general x1, local copies, waits for them, and re-layouts, on_device(): jnp.einsum('absp,spxy->axby', landing, incoming, precision=largest_index)  34.4 us
    another operation x6, other arithmetic, on_device(): factor = jnp.linalg.cholesky(jnp.where(at_root, corner, identity))  34 us
  transfers between devices with their start and end apart: 5, of which 4 were waited for; matrix products, arithmetic and copies ran while one was open for 8% of the time, Pallas kernels for 0%

commit v1 on v0

--- a/solution.py
+++ b/solution.py
@@ -6,7 +6,7 @@
 
 def broadcast(value, axis, source):
     kept = jnp.where(lax.axis_index(axis) == source, value, 0).astype(value.dtype)
-    return lax.psum(kept, axis)
+    return jnp.sum(lax.all_gather(kept, axis), axis=0)
 
 
 def slot_positions(owners, is_live):

time: 1480 us -> 1960 us (1.32)
  waiting for transfers between devices: 910 us -> 1370 us
    all_gather x0 -> x2, waiting for transfers between devices: none -> 637 us  [broadcast(): return jnp.sum(lax.all_gather(kept, axis), axis=0)]
    psum x2 -> x0, waiting for transfers between devices: 171 us -> none  [broadcast(): return lax.psum(kept, axis)]
    unnamed x26 -> x25, local copies, waits for them, and re-layouts: 33.2 us -> 39.3 us
  transfers between devices with their start and end apart: 5 -> 5, of which waited for: 4 -> 3; matrix products, arithmetic and copies ran while one was open for 8% -> 7% of each run, Pallas kernels for 0% -> 0%
where the time goes in v1:
time: 1960 us; the launch traced here: 1950 us
  waiting for transfers between devices  1370 us (70%)
  local copies, waits for them, and re-layouts  279 us (14%)
  other arithmetic  177 us (9%)
  matrix products  83.7 us (4%)
    all_to_all x1, waiting for transfers between devices, on_device(): lax.all_to_all(front_panels, 'col', split_axis=4, concat_axis=2, tiled=True)  637 us
    all_gather x2, waiting for transfers between devices, broadcast(): return jnp.sum(lax.all_gather(kept, axis), axis=0)  637 us
    all_gather x1, waiting for transfers between devices, on_device(): whole = lax.all_gather(row_panel, 'row', axis=0, tiled=True)  94.7 us
    reshape x1, local copies, waits for them, and re-layouts, on_device(): return blocks.reshape(row_tiles, 1, front_width, col_tiles, 1, front_width)  78.3 us
    unnamed x25, local copies, waits for them, and re-layouts  39.3 us
  transfers between devices with their start and end apart: 5, of which 3 were waited for; matrix products, arithmetic and copies ran while one was open for 7% of the time, Pallas kernels for 0%

profile of v1, /device:TPU:0, one launch (start us, length us, event | category | flops | bytes accessed | tf_op | source)
XLA Modules:
  0.0 1951.1 jit_solution(7079363778250343675)
XLA Ops:
  19.8 4.2 all-to-all-start.1
  24.0 30.6 %copy.71 = f32[16,1,32,8,8,256]{5,3,2,0,1,4:T(8,128)} copy(f32[16,1,32,8,8,256]{5,4,3,2,1,0:T(8,128)} %param.9) | data formatting | bytes 67108864 | tf_op args[0]
  55.9 7.1 all-to-all-start
  64.4 5.8 all-reduce.1
  70.2 5.0 all_gather.24
  75.3 5.2 all_gather.27
  85.0 30.9 %convolution_bitcast_fusion = f32[256,256,16,8]{1,2,3,0:T(8,128)} fusion(f32[4,2,256,256,1]{3,2,1,0,4:T(8,128)S(1)} %bitcast.108, f32[16,8,4,2]{0,1,3,2:T(8,128)S(1)} %convolution_bitcast_fusion.1), kind=kOutput, calls=%fused_computation.8 | convolution fusion | flops 805306368 | bytes 35655680 | tf_op jit(solution)/shard_map/absp,spxy->axby/dot_general | solution.py:95
  116.0 34.4 %copy.76 = f32[256,256,16,8]{0,1,3,2:T(8,128)} copy(f32[256,256,16,8]{1,2,3,0:T(8,128)} %convolution_bitcast_fusion) | data formatting | bytes 67108864 | tf_op jit(solution)/shard_map/absp,spxy->axby/dot_general | solution.py:95
  150.4 637.4 %all-to-all-done = f32[16,1,32,8,8,256]{5,3,2,0,1,4:T(8,128)} async-done(((f32[16,1,32,8,8,256]{5,3,2,0,1,4:T(8,128)}), f32[16,1,32,8,8,256]{5,3,2,0,1,4:T(8,128)}, u32[]{:S(2)}, u32[]{:S(2)}) %all-to-all-start) | async-done | bytes 33554464 | tf_op jit(solution)/shard_map/all_to_all | solution.py:30
  787.8 22.9 %copy.72 = f32[16,1,32,8,8,256]{5,3,2,4,0,1:T(8,128)} copy(f32[16,1,32,8,8,256]{5,3,2,0,1,4:T(8,128)} %all-to-all-done) | data formatting | bytes 67108864 | tf_op jit(solution)/shard_map/all_to_all | solution.py:30
  810.7 35.0 %copy.77 = f32[16,256,8,256]{1,3,2,0:T(8,128)} copy(f32[16,256,8,256]{3,2,1,0:T(8,128)} %bitcast.101) | data formatting | bytes 67108864 | tf_op jit(solution)/shard_map/reshape | solution.py:33
  845.7 33.5 %bitcast_add_fusion.1 = f32[16,256,8,256]{1,3,2,0:T(8,128)} fusion(f32[16,256,8,256]{1,3,2,0:T(8,128)} %copy.77, f32[256,256,16,8]{0,1,3,2:T(8,128)} %copy.76), kind=kLoop, calls=%fused_computation.5 | loop fusion | flops 8388608 | bytes 100663296 | tf_op jit(solution)/shard_map/add | solution.py:95
  879.2 31.9 %copy.78 = f32[16,256,8,256]{3,1,2,0:T(8,128)} copy(f32[16,256,8,256]{1,3,2,0:T(8,128)} %bitcast_add_fusion.1) | data formatting | bytes 67108864 | tf_op jit(solution)/shard_map/add | solution.py:95
  911.2 33.6 %fusion.1 = f32[16,256,8,256]{1,3,2,0:T(8,128)} fusion(f32[16,256,8,256]{1,3,2,0:T(8,128)} %bitcast_add_fusion.1, f32[16,256,8,256]{3,1,2,0:T(8,128)} %copy.78, pred[16,8]{1,0:T(8,128)(4,1)S(1)} %get-tuple-element.42), kind=kLoop, calls=%fused_computation.4 | loop fusion | flops 25165824 | bytes 100663424 | tf_op jit(solution)/shard_map/jit(_where)/select_n | solution.py:99
  946.9 11.7 cholesky.50
  958.7 9.8 custom-call.15
  969.0 11.7 cholesky.105
  983.6 4.5 slice.96
  988.1 5.8 copy.80
  993.9 5.6 copy.81
  1004.9 19.7 %custom-call.16 = f32[2,128,128]{1,2,0:T(8,128)S(1)} custom-call(f32[2,128,128]{2,1,0:T(8,128)S(1)} %get-tuple-element.24), custom_call_target="InvertDiagBlocksLowerTriangular" | custom-call | tf_op jit(solution)/shard_map/jit(_solve_triangular)/triangular_solve | solution.py:106
  1034.5 5.6 copy.101
  1040.1 4.7 select_select_fusion
  1044.9 637.1 %all-gather.5.cloned.1.call-done = f32[8,16,256,256]{3,2,1,0:T(8,128)} async-done(((f32[1,16,256,256]{3,2,1,0:T(8,128)}), f32[8,16,256,256]{3,2,1,0:T(8,128)}) %all-gather.5.cloned.1.call-update) | async-done | bytes 33554448 | tf_op jit(solution)/shard_map/all_gather | solution.py:9
  1682.0 14.4 reduce_sum.39
  1696.6 5.4 copy.90
  1702.0 5.9 copy.104
  1707.9 94.7 %all-gather.7.cloned.1.call-done = f32[64,256,256]{2,1,0:T(8,128)} async-done(((f32[16,256,256]{2,1,0:T(8,128)}), f32[64,256,256]{2,1,0:T(8,128)}) %all-gather.7.cloned.1.call-update) | async-done | bytes 16777232 | tf_op jit(solution)/shard_map/all_gather | solution.py:114
  1802.5 35.7 %convolution_subtract_fusion = f32[16,256,8,256]{1,3,2,0:T(8,128)} fusion(f32[16,256,8,256]{1,3,2,0:T(8,128)} %fusion.1, f32[16,256,256,1]{1,0,2,3:T(8,128)} %bitcast.104, f32[4,8,2,256,256]{4,3,2,1,0:T(8,128)} %bitcast.110, s32[]{:T(128)S(6)} %select_n.153, s32[]{:T(128)S(6)} %select_n.156), kind=kOutput, calls=%fused_computation.7 | convolution fusion | flops 25778192384 | bytes 73400328 | tf_op jit(solution)/shard_map/asx,bqx->asbq/dot_general | solution.py:118
  1838.3 4.8 fusion.2
  1843.1 22.9 %select_bitcast_fusion = f32[16,1,256,8,1,256]{2,5,3,0,4,1:T(8,128)} fusion(f32[16,256,8,256]{1,3,2,0:T(8,128)} %fusion.2, pred[16,8]{1,0:T(8,128)(4,1)S(1)} %copy-done.5), kind=kLoop, calls=%fused_computation.6 | loop fusion | flops 8388608 | bytes 67108992 | tf_op jit(solution)/shard_map/reshape | solution.py:122
  1866.0 78.3 %copy.91 = f32[16,1,256,8,1,256]{5,4,3,2,1,0:T(1,128)} copy(f32[16,1,256,8,1,256]{2,5,3,0,4,1:T(8,128)} %select_bitcast_fusion) | data formatting | bytes 67108864 | tf_op jit(solution)/shard_map/reshape | solution.py:122
  (81 shorter events, 43.3 us)
Async XLA Ops:
  6.5 1.6 copy-start
  6.5 3.8 copy-start.6
  19.8 34.8 %all-to-all-start.1 = ((f32[4,2,65536]{2,1,0:T(2,128)}), f32[4,2,65536]{2,1,0:T(2,128)S(1)}, u32[]{:S(2)}, u32[]{:S(2)}) async-start(f32[4,2,65536]{2,1,0:T(2,128)} %fusion.33), calls=%async_computation.1 | async-start | bytes 4194304 | tf_op jit(solution)/shard_map/all_to_all | solution.py:69
  54.6 8.5 copy-start.9
  54.6 15.7 copy-start.7
  54.6 20.7 %copy-start.8 = (s32[1,1,8]{2,1,0:T(1,128)S(1)}, s32[1,1,8]{2,1,0:T(1,128)}, u32[]{:S(2)}) copy-start(s32[1,1,8]{2,1,0:T(1,128)} %param.12) | copy-start | bytes 100
  54.6 1.3 copy-start.4
  55.9 731.9 %all-to-all-start = ((f32[16,1,32,8,8,256]{5,3,2,0,1,4:T(8,128)}), f32[16,1,32,8,8,256]{5,3,2,0,1,4:T(8,128)}, u32[]{:S(2)}, u32[]{:S(2)}) async-start(f32[16,1,32,8,8,256]{5,3,2,0,1,4:T(8,128)} %copy.71), calls=%async_computation | async-start | bytes 67108864 | tf_op jit(solution)/shard_map/all_to_all | solution.py:30
  63.0 936.6 %all-gather.9.cloned.1.call-start = ((), (), s32[]{:S(2)}) async-start(), calls=%async_computation.4 | async-start | bytes 1310720 | tf_op jit(solution)/shard_map/all_gather | solution.py:9
  983.5 698.5 %all-gather.5.cloned.1.call-start = ((), (), s32[]{:S(2)}) async-start(), calls=%async_computation.2 | async-start | bytes 37748736 | tf_op jit(solution)/shard_map/all_gather | solution.py:9
  1024.6 3.7 copy-start.3
  1044.8 757.7 %all-gather.7.cloned.1.call-start = ((), (), s32[]{:S(2)}) async-start(), calls=%async_computation.3 | async-start | bytes 20971520 | tf_op jit(solution)/shard_map/all_gather | solution.py:114
  1802.5 35.7 %copy-start.2 = (f32[16,256,1,256]{1,3,2,0:T(8,128)S(1)}, f32[16,256,1,256]{1,3,2,0:T(8,128)}, u32[]{:S(2)}) copy-start(f32[16,256,1,256]{1,3,2,0:T(8,128)} %copy.90) | copy-start | bytes 12582916
  1838.3 4.8 copy-start.5
  1866.0 78.3 %copy-start.1 = (f32[1,1,8,256,256]{4,3,2,1,0:T(8,128)S(1)}, f32[1,1,8,256,256]{4,3,2,1,0:T(8,128)}, u32[]{:S(2)}) copy-start(f32[1,1,8,256,256]{4,3,2,1,0:T(8,128)} %param.10) | copy-start | bytes 6291460
Sparse Core Ops, SparseCore 0:
  983.6 15.1 all-gather.8
  1045.0 637.0 all-gather.4
  1696.6 105.8 all-gather.6
